TPU v7x, 32 devices: a whole 2x2x4 slice. The times are simulated.
32 devices in a mesh: groups: 2 (over y), edge: 4 (over z), expert: 2 (over x), sys: 2 (over core).
Axes of the slice: x: 2, y: 2, z: 4, core: 2. Of those that a mesh axis runs over, the one named last changes fastest.
Arguments:
- edge_inputs: bfloat16 [8, 1792, 1280], P(('groups', 'expert', 'sys'), 'edge'), parts along dimension 0, may hold values from -6 to 6
- out_grad: bfloat16 [8, 1792, 1152], P(('groups', 'expert', 'sys'), 'edge'), parts along dimension 0, may hold values from -6 to 6
- expert_weights: bfloat16 [32, 1280, 1152], P('expert', 'edge'), may hold values from -0.15625 to 0.15625
- coef_table: float32 [16, 32], replicated, may hold values from 0.05 to 0.5
- system_kind: int32 [8], P('groups'), parts along dimension 0, may hold values from 0 to 15
- edge_counts: int32 [8], P('groups'), parts along dimension 0, may hold values from 896 to 1792, as said below
Outputs:
- input_grad: bfloat16 [8, 1792, 1280], P(('groups', 'expert', 'sys'), 'edge'), parts along dimension 0
- weight_grad: bfloat16 [64, 1280, 1152], P(('groups', 'expert'), 'edge'), parts along dimension 0
There are 2 independent parts, one for each index of `groups`. A program takes and returns all parts, laid end to end along the dimension named above; an argument that names none is the same for every part. Nothing has to cross between parts.
Inputs may be any that keep to these rules, and one draw needn't show every extreme that they name: `edge_counts`: the live edges of a system are its first ones. One system has all 1792 slots live and another exactly half of them.
All inputs are finite; a program needn't handle non-finite values.
Results may differ from a plain program's by a relative error of at most 0.018.
Values may be sent and summed in bfloat16 or wider, within the bound.
No kernel may reach another device: no remote copies, remote signals or barrier semaphores. Data moves between devices by JAX's collectives and lax.ppermute only.
A program may use at most 128 MiB of HBM per device.

v0:
```python
import math
import jax
import jax.numpy as jnp
from jax import lax
from jax.sharding import PartitionSpec as P


def body(edge_inputs, out_grad, expert_weights, coef_table, system_kind, edge_counts):
    highest = lax.Precision.HIGHEST
    edge_size = lax.axis_size("edge")
    expert_size = lax.axis_size("expert")
    sys_size = lax.axis_size("sys")
    edge_at = lax.axis_index("edge")
    expert_at = lax.axis_index("expert")
    sys_at = lax.axis_index("sys")
    systems = system_kind.shape[0]
    kinds = coef_table.shape[0]
    exp_local = expert_weights.shape[0]
    row_count = expert_weights.shape[1]
    width_out = expert_weights.shape[2]
    edge_rows = out_grad.shape[1]
    onehot = (system_kind[:, None] == jnp.arange(kinds, dtype=jnp.int32)[None, :]).astype(
        jnp.float32
    )
    coeffs = jnp.dot(onehot, coef_table, precision=highest)
    own_system = expert_at * sys_size + sys_at
    picked = jnp.arange(systems, dtype=jnp.int32) == own_system
    own_count = jnp.sum(jnp.where(picked, edge_counts, 0))
    positions = edge_at * edge_rows + jnp.arange(edge_rows, dtype=jnp.int32)
    masked_grad = jnp.where(
        (positions < own_count)[:, None], out_grad[0], jnp.zeros((), jnp.bfloat16)
    )
    features = edge_inputs[0]
    by_block = coeffs.reshape(expert_size, sys_size, -1)
    same_sys = lax.dynamic_slice_in_dim(by_block, sys_at, 1, 1)[:, 0, :]
    own_coeffs = lax.dynamic_slice_in_dim(same_sys, expert_at * exp_local, exp_local, 1)
    partials = jnp.sum(
        own_coeffs[:, :, None, None] * expert_weights.astype(jnp.float32)[None], axis=1
    ).astype(jnp.bfloat16)
    merged_rows = jnp.sum(
        lax.all_to_all(partials, "expert", split_axis=0, concat_axis=0, tiled=True).astype(
            jnp.float32
        ),
        axis=0,
    ).astype(jnp.bfloat16)
    product = lax.dot_general(
        masked_grad,
        lax.all_gather(merged_rows, "edge", axis=0, tiled=True),
        (((1,), (1,)), ((), ())),
        preferred_element_type=jnp.float32,
    )
    input_grad = product.astype(jnp.bfloat16)
    system_rows = lax.psum_scatter(
        lax.dot_general(
            features, masked_grad, (((0,), (0,)), ((), ())), preferred_element_type=jnp.float32
        ).astype(jnp.bfloat16),
        "edge",
        scatter_dimension=0,
        tiled=True,
    )
    local_coeffs = lax.dynamic_slice_in_dim(coeffs, expert_at * exp_local, exp_local, 1).T
    block_rows = lax.all_gather(system_rows[None], ("expert", "sys"), axis=0, tiled=True)
    span_rows = block_rows.shape[0]
    flat_rows = block_rows.reshape(span_rows, -1).astype(jnp.float32)
    folded = jnp.dot(local_coeffs, flat_rows, precision=highest)
    scale_factor = 1.0 / math.sqrt(edge_rows * edge_size)
    weight_grad = (
        (folded * scale_factor).reshape(exp_local, row_count, width_out).astype(jnp.bfloat16)
    )
    return (input_grad[None], weight_grad)


def solution(mesh):
    return jax.shard_map(
        body,
        mesh=mesh,
        in_specs=(
            P(("groups", "expert", "sys"), "edge", None),
            P(("groups", "expert", "sys"), "edge", None),
            P("expert", "edge", None),
            P(),
            P("groups"),
            P("groups"),
        ),
        out_specs=(
            P(("groups", "expert", "sys"), "edge", None),
            P(("groups", "expert"), "edge", None),
        ),
        check_vma=False,
    )
```

profile of v0, /device:TPU:0, one launch (start us, length us, event | category | flops | bytes accessed | tf_op | source)
XLA Modules:
  0.0 198.3 jit_solution(15670721173112743282)
XLA Ops:
  7.2 0.0 copy-start
  7.2 0.0 reduce-scatter.4.cloned.1.call-start
  7.2 1.4 fusion.13
  8.6 0.7 add_compare_fusion
  9.3 4.7 %fusion.1 = bf16[1280,1152]{0,1:T(8,128)(2,1)} fusion(bf16[1,448,1280]{2,1,0:T(8,128)(2,1)S(1)} %copy-done, bf16[1,448,1152]{2,1,0:T(8,128)(2,1)} %param.7, pred[448]{0:T(512)(128)(4,1)S(1)} %add_compare_fusion), kind=kOutput, calls=%fused_computation.4 | convolution fusion | flops 1323196416 | bytes 5128640 | tf_op jit(solution)/shard_map/dot_general | solution.py:54
  13.9 5.4 %copy.11 = bf16[1280,1152]{1,0:T(8,128)(2,1)} copy(bf16[1280,1152]{0,1:T(8,128)(2,1)} %fusion.1) | data formatting | bytes 5898240
  19.4 0.0 reduce-scatter.4.cloned.1.call-update
  19.4 0.0 all-gather.4.cloned.1.call-start
  19.5 13.6 %convert_element_type.25 = f32[16,320,1152]{2,1,0:T(8,128)} convert(bf16[16,320,1152]{2,1,0:T(8,128)(2,1)} %param.8) | non-fusion elementwise | flops 5898240 | bytes 35389440 | tf_op jit(solution)/shard_map/convert_element_type | solution.py:38
  33.1 0.2 fusion.11
  33.3 0.1 constant_dynamic-slice_fusion
  33.4 13.5 %multiply_reduce_fusion = bf16[2,320,1152]{2,1,0:T(8,128)(2,1)S(1)} fusion(f32[16,320,1152]{2,1,0:T(8,128)} %convert_element_type.25, f32[2,16]{1,0:T(2,128)S(1)} %bitcast.24), kind=kLoop, calls=%fused_computation.2 | loop fusion | flops 22855680 | bytes 25067648 | tf_op jit(solution)/shard_map/reduce_sum | solution.py:37
  46.9 22.3 %all_to_all.5 = bf16[2,320,1152]{2,1,0:T(8,128)(2,1)S(1)} all-to-all(bf16[2,320,1152]{2,1,0:T(8,128)(2,1)S(1)} %multiply_reduce_fusion), channel_id=1, replica_groups=mesh['groups'=2,'edge'=4,'expert'=2,'sys'=2] {'expert'}, dimensions={0} | all-to-all | bytes 2949120 | tf_op jit(solution)/shard_map/all_to_all | solution.py:41
  69.2 1.3 reduce_sum.32
  70.5 0.0 all-gather.4.cloned.1.call-update
  70.5 0.0 all-gather.6.cloned.1.call-start
  70.6 9.0 %reduce-scatter.4.cloned.1.call-done = bf16[320,1152]{1,0:T(8,128)(2,1)} async-done(((bf16[1280,1152]{1,0:T(8,128)(2,1)}), bf16[320,1152]{1,0:T(8,128)(2,1)}) %reduce-scatter.4.cloned.1.call-update) | async-done | bytes 737296 | tf_op jit(solution)/shard_map/reduce_scatter | solution.py:53
  79.6 0.0 all-gather.6.cloned.1.call-update
  79.7 62.1 %all-gather.4.cloned.1.call-done = bf16[1280,1152]{1,0:T(8,128)(2,1)} async-done(((bf16[320,1152]{1,0:T(8,128)(2,1)}), bf16[1280,1152]{1,0:T(8,128)(2,1)}) %all-gather.4.cloned.1.call-update) | async-done | bytes 2949136 | tf_op jit(solution)/shard_map/all_gather | solution.py:48
  141.8 4.6 %fusion.2 = bf16[1,448,1280]{2,1,0:T(8,128)(2,1)} fusion(bf16[1280,1152]{1,0:T(8,128)(2,1)} %all-gather.4.cloned.1.call-done, bf16[1,448,1152]{2,1,0:T(8,128)(2,1)S(1)} %copy-done.2, pred[448]{0:T(512)(128)(4,1)S(1)} %add_compare_fusion), kind=kOutput, calls=%fused_computation.6 | convolution fusion | flops 1322295296 | bytes 5128640 | tf_op jit(solution)/shard_map/dot_general | solution.py:46
  146.3 23.1 %all-gather.6.cloned.1.call-done = bf16[1280,1152]{1,0:T(8,128)(2,1)} async-done(((bf16[320,1152]{1,0:T(8,128)(2,1)}), bf16[1280,1152]{1,0:T(8,128)(2,1)}) %all-gather.6.cloned.1.call-update) | async-done | bytes 2949136 | tf_op jit(solution)/shard_map/all_gather | solution.py:62
  169.4 4.5 %reshape.31 = bf16[4,368640]{1,0:T(4,128)(2,1)} reshape(bf16[1280,1152]{1,0:T(8,128)(2,1)} %all-gather.6.cloned.1.call-done) | data formatting | bytes 5898240 | tf_op jit(solution)/shard_map/reshape | solution.py:64
  173.9 12.6 %fusion = bf16[16,368640]{1,0:T(8,128)(2,1)S(1)} fusion(bf16[4,368640]{1,0:T(4,128)(2,1)} %reshape.31, f32[4,32]{1,0:T(4,128)S(1)} %fusion.11, s32[]{:T(128)S(6)} %select_n.28), kind=kOutput, calls=%fused_computation.1 | convolution fusion | flops 294912000 | bytes 14746116 | tf_op jit(solution)/shard_map/dot_general | solution.py:65
  186.6 5.3 %copy.13 = bf16[2,8,320,1152]{3,2,1,0:T(8,128)(2,1)} copy(bf16[2,8,320,1152]{3,1,2,0:T(8,128)(2,1)S(1)} %bitcast.21) | data formatting | bytes 23592960
  (9 shorter events, 0.0 us)
Async XLA Ops:
  7.2 2.1 %copy-start = (bf16[1,448,1280]{2,1,0:T(8,128)(2,1)S(1)}, bf16[1,448,1280]{2,1,0:T(8,128)(2,1)}, u32[]{:S(2)}) copy-start(bf16[1,448,1280]{2,1,0:T(8,128)(2,1)} %param.6) | copy-start | bytes 3440644
  7.2 72.5 %reduce-scatter.4.cloned.1.call-start = ((), (), s32[]{:S(2)}) async-start(), calls=%async_computation.4 | async-start | bytes 3686400 | tf_op jit(solution)/shard_map/reduce_scatter | solution.py:53
  19.4 122.4 %all-gather.4.cloned.1.call-start = ((), (), s32[]{:S(2)}) async-start(), calls=%async_computation.2 | async-start | bytes 3686400 | tf_op jit(solution)/shard_map/all_gather | solution.py:48
  19.5 13.7 %copy-start.3 = (f32[16,32]{1,0:T(8,128)S(1)}, f32[16,32]{1,0:T(8,128)}, u32[]{:S(2)}) copy-start(f32[16,32]{1,0:T(8,128)} %param.9) | copy-start | bytes 6148
  19.5 13.7 %copy-start.4 = (s32[4]{0:T(128)S(1)}, s32[4]{0:T(128)}, u32[]{:S(2)}) copy-start(s32[4]{0:T(128)} %param.10) | copy-start | bytes 52
  46.8 94.9 %copy-start.2 = (bf16[1,448,1152]{2,1,0:T(8,128)(2,1)S(1)}, bf16[1,448,1152]{2,1,0:T(8,128)(2,1)}, u32[]{:S(2)}) copy-start(bf16[1,448,1152]{2,1,0:T(8,128)(2,1)} %param.7) | copy-start | bytes 3096580
  70.5 98.9 %all-gather.6.cloned.1.call-start = ((), (), s32[]{:S(2)}) async-start(), calls=%async_computation.3 | async-start | bytes 3686400 | tf_op jit(solution)/shard_map/all_gather | solution.py:62
  186.5 5.3 %copy-start.1 = (bf16[1,448,1280]{2,1,0:T(8,128)(2,1)S(1)}, bf16[1,448,1280]{2,1,0:T(8,128)(2,1)}, u32[]{:S(2)}) copy-start(bf16[1,448,1280]{2,1,0:T(8,128)(2,1)} %param.6) | copy-start | bytes 3440644
Sparse Core Ops, SparseCore 0:
  19.5 60.0 reduce-scatter.3
  81.8 59.9 all-gather.3
  143.3 26.0 all-gather.5
where the time goes:
time: 199 us; the launch traced here: 198 us
  waiting for transfers between devices  94.3 us (47%)
  other arithmetic  30.4 us (15%)
  blocking collectives  22.3 us (11%)
  matrix products  22 us (11%)
  local copies, waits for them, and re-layouts  15.3 us (8%)
  between operations  13.8 us (7%)
    all_gather x1, waiting for transfers between devices, body(): lax.all_gather(merged_rows, 'edge', axis=0, tiled=True)  62.1 us
    all_gather x1, waiting for transfers between devices, body(): lax.all_gather(system_rows[None], ('expert', 'sys'), axis=0, tiled=True)  23.1 us
    all_to_all x1, blocking collectives, body(): lax.all_to_all(partials, 'expert', split_axis=0, concat_axis=0, tiled=True)  22.3 us
    convert_element_type x1, other arithmetic, body(): expert_weights.astype(jnp.float32)[None]  13.6 us
    reduce_sum x1, other arithmetic, body(): jnp.sum(own_coeffs[:, :, None, None] * expert_weights.astype(jnp.float32)...  13.5 us
    dot_general x1, matrix products, body(): folded = jnp.dot(local_coeffs, flat_rows, precision=highest)  12.6 us
    unnamed x12, local copies, waits for them, and re-layouts  10.7 us
    reduce_scatter x1, waiting for transfers between devices, body(): lax.psum_scatter(lax.dot_general(features, masked_grad, (((0,), (0,)), ((...  9.04 us
  transfers between devices with their start and end apart: 3, of which 3 were waited for; matrix products, arithmetic and copies ran while one was open for 17% of the time, Pallas kernels for 0%

commit v1 on v0

--- a/solution.py
+++ b/solution.py
@@ -59,7 +59,32 @@
         tiled=True,
     )
     local_coeffs = lax.dynamic_slice_in_dim(coeffs, expert_at * exp_local, exp_local, 1).T
-    block_rows = lax.all_gather(system_rows[None], ("expert", "sys"), axis=0, tiled=True)
+    length, place, width = (
+        lax.axis_size(("expert", "sys")),
+        lax.axis_index(("expert", "sys")),
+        system_rows[None].shape[0],
+    )
+    upward = [(i, (i + 1) % length) for i in range(length)]
+    left = [(i, (i - 1) % length) for i in range(length)]
+    block_rows = jnp.zeros(
+        (*system_rows[None].shape[:0], length * width, *system_rows[None].shape[0 + 1 :]),
+        system_rows[None].dtype,
+    )
+    block_rows = lax.dynamic_update_slice_in_dim(
+        block_rows, system_rows[None], place * width, axis=0
+    )
+    from_left = from_right = system_rows[None]
+    halfway = length // 2
+    for step in range(1, halfway + 1):
+        from_left = lax.ppermute(from_left, ("expert", "sys"), upward)
+        block_rows = lax.dynamic_update_slice_in_dim(
+            block_rows, from_left, (place - step) % length * width, axis=0
+        )
+        if step < length - halfway:
+            from_right = lax.ppermute(from_right, ("expert", "sys"), left)
+            block_rows = lax.dynamic_update_slice_in_dim(
+                block_rows, from_right, (place + step) % length * width, axis=0
+            )
     span_rows = block_rows.shape[0]
     flat_rows = block_rows.reshape(span_rows, -1).astype(jnp.float32)
     folded = jnp.dot(local_coeffs, flat_rows, precision=highest)

time: 199 us -> 184 us (0.925)
  waiting for transfers between devices: 94.3 us -> 77.4 us
    all_gather x1 -> x0, waiting for transfers between devices: 23.1 us -> none  [body(): lax.all_gather(system_rows[None], ('expert', 'sys'), axis=0, tiled=True)]
    ppermute x0 -> x3, waiting for transfers between devices: none -> 10.3 us  [the longest x2 10.3 us: body(): from_left = lax.ppermute(from_left, ('expert', 'sys'), upward)]
    unnamed x3, waiting for transfers between devices: 0.05 us -> 9.34 us
    reduce_scatter x1 -> x0, waiting for transfers between devices: 9.04 us -> none  [body(): lax.psum_scatter(lax.dot_general(features, masked_grad, (((0,), (0,)), ((...]
    reshape x1 -> x0, local copies, waits for them, and re-layouts: 4.52 us -> none  [body(): flat_rows = block_rows.reshape(span_rows, -1).astype(jnp.float32)]
    all_gather x1, waiting for transfers between devices: 62.1 us -> 57.8 us  [body(): lax.all_gather(merged_rows, 'edge', axis=0, tiled=True)]
    unnamed x12, local copies, waits for them, and re-layouts: 10.7 us -> 14.7 us
  transfers between devices with their start and end apart: 3 -> 5, of which waited for: 3 -> 3; matrix products, arithmetic and copies ran while one was open for 17% -> 20% of each run, Pallas kernels for 0% -> 0%
where the time goes in v1:
time: 184 us; the launch traced here: 183 us
  waiting for transfers between devices  77.4 us (42%)
  other arithmetic  30.4 us (17%)
  blocking collectives  22.2 us (12%)
  matrix products  20.9 us (11%)
  local copies, waits for them, and re-layouts  16.2 us (9%)
  between operations  14.2 us (8%)
    all_gather x1, waiting for transfers between devices, body(): lax.all_gather(merged_rows, 'edge', axis=0, tiled=True)  57.8 us
    all_to_all x1, blocking collectives, body(): lax.all_to_all(partials, 'expert', split_axis=0, concat_axis=0, tiled=True)  22.2 us
    unnamed x12, local copies, waits for them, and re-layouts  14.7 us
    convert_element_type x1, other arithmetic, body(): expert_weights.astype(jnp.float32)[None]  13.6 us
    reduce_sum x1, other arithmetic, body(): jnp.sum(own_coeffs[:, :, None, None] * expert_weights.astype(jnp.float32)...  13.5 us
    dot_general x1, matrix products, body(): folded = jnp.dot(local_coeffs, flat_rows, precision=highest)  11.2 us
    ppermute x2, waiting for transfers between devices, body(): from_left = lax.ppermute(from_left, ('expert', 'sys'), upward)  10.3 us
    unnamed x3, waiting for transfers between devices  9.34 us
  transfers between devices with their start and end apart: 5, of which 3 were waited for; matrix products, arithmetic and copies ran while one was open for 20% of the time, Pallas kernels for 0%

profile of v1, /device:TPU:0, one launch (start us, length us, event | category | flops | bytes accessed | tf_op | source)
XLA Modules:
  0.0 183.2 jit_solution(14726288306122678465)
XLA Ops:
  7.2 1.4 fusion.14
  8.6 0.7 add_compare_fusion
  9.3 4.6 %fusion.1 = bf16[1280,1152]{0,1:T(8,128)(2,1)} fusion(bf16[1,448,1280]{2,1,0:T(8,128)(2,1)S(1)} %copy-done, bf16[1,448,1152]{2,1,0:T(8,128)(2,1)} %param.7, pred[448]{0:T(512)(128)(4,1)S(1)} %add_compare_fusion), kind=kOutput, calls=%fused_computation.4 | convolution fusion | flops 1323196416 | bytes 5128640 | tf_op jit(solution)/shard_map/dot_general | solution.py:54
  13.9 5.4 %copy.18 = bf16[1280,1152]{1,0:T(8,128)(2,1)} copy(bf16[1280,1152]{0,1:T(8,128)(2,1)} %fusion.1) | data formatting | bytes 5898240
  19.5 13.6 %convert_element_type.25 = f32[16,320,1152]{2,1,0:T(8,128)} convert(bf16[16,320,1152]{2,1,0:T(8,128)(2,1)} %param.8) | non-fusion elementwise | flops 5898240 | bytes 35389440 | tf_op jit(solution)/shard_map/convert_element_type | solution.py:38
  33.1 0.2 fusion.11
  33.3 13.5 %multiply_reduce_fusion = bf16[2,320,1152]{2,1,0:T(8,128)(2,1)S(1)} fusion(f32[16,320,1152]{2,1,0:T(8,128)} %convert_element_type.25, f32[2,16]{1,0:T(2,128)S(1)} %bitcast.30), kind=kLoop, calls=%fused_computation.2 | loop fusion | flops 22855680 | bytes 25067648 | tf_op jit(solution)/shard_map/reduce_sum | solution.py:37
  46.8 22.2 %all_to_all.5 = bf16[2,320,1152]{2,1,0:T(8,128)(2,1)S(1)} all-to-all(bf16[2,320,1152]{2,1,0:T(8,128)(2,1)S(1)} %multiply_reduce_fusion), channel_id=1, replica_groups=mesh['groups'=2,'edge'=4,'expert'=2,'sys'=2] {'expert'}, dimensions={0} | all-to-all | bytes 2949120 | tf_op jit(solution)/shard_map/all_to_all | solution.py:41
  69.0 1.3 reduce_sum.32
  70.3 9.3 %reduce-scatter.4.cloned.1.call-done = bf16[320,1152]{1,0:T(8,128)(2,1)} async-done(((bf16[1280,1152]{1,0:T(8,128)(2,1)}), bf16[320,1152]{1,0:T(8,128)(2,1)}) %reduce-scatter.4.cloned.1.call-update) | async-done | bytes 737296
  79.6 1.7 copy.19
  81.4 0.8 copy.15
  82.3 1.7 collective-permute-start.1
  84.0 57.8 %all-gather.2.cloned.1.call-done = bf16[1280,1152]{1,0:T(8,128)(2,1)} async-done(((bf16[320,1152]{1,0:T(8,128)(2,1)}), bf16[1280,1152]{1,0:T(8,128)(2,1)}) %all-gather.2.cloned.1.call-update) | async-done | bytes 2949136 | tf_op jit(solution)/shard_map/all_gather | solution.py:48
  141.8 4.9 %fusion.2 = bf16[1,448,1280]{2,1,0:T(8,128)(2,1)} fusion(bf16[1280,1152]{1,0:T(8,128)(2,1)} %all-gather.2.cloned.1.call-done, bf16[1,448,1152]{2,1,0:T(8,128)(2,1)} %param.7, pred[448]{0:T(512)(128)(4,1)S(1)} %add_compare_fusion), kind=kOutput, calls=%fused_computation.6 | convolution fusion | flops 1322295296 | bytes 5128640 | tf_op jit(solution)/shard_map/dot_general | solution.py:46
  146.6 0.2 broadcast_in_dim.39
  146.9 0.1 constant_dynamic-update-slice_fusion.3
  147.0 0.1 constant_dynamic-update-slice_fusion.2
  147.1 0.1 constant_dynamic-update-slice_fusion.1
  147.2 10.3 %collective-permute-done.2 = bf16[1,320,1152]{2,1,0:T(8,128)(2,1)S(1)} collective-permute-done((bf16[1,320,1152]{2,1,0:T(8,128)(2,1)S(1)}, bf16[1,320,1152]{2,1,0:T(8,128)(2,1)S(1)}, u32[]{:S(2)}, u32[]{:S(2)}) %collective-permute-start.2) | collective-permute-done | bytes 737312 | tf_op jit(solution)/shard_map/ppermute | solution.py:79
  157.5 0.1 constant_dynamic-update-slice_fusion
  157.6 2.3 %copy.20 = bf16[1,4,320,1152]{3,1,2,0:T(4,128)(2,1)S(1)} copy(bf16[1,4,320,1152]{3,2,1,0:T(8,128)(2,1)S(1)} %bitcast.27) | data formatting | bytes 5898240
  159.9 11.2 %fusion = bf16[16,368640]{1,0:T(8,128)(2,1)S(1)} fusion(bf16[4,368640]{1,0:T(4,128)(2,1)S(1)} %bitcast.25, f32[4,32]{1,0:T(4,128)S(1)} %fusion.11, s32[]{:T(128)S(6)} %select_n.55), kind=kOutput, calls=%fused_computation.1 | convolution fusion | flops 294912000 | bytes 14746116 | tf_op jit(solution)/shard_map/dot_general | solution.py:90
  171.1 5.3 %copy.21 = bf16[2,8,320,1152]{3,2,1,0:T(8,128)(2,1)} copy(bf16[2,8,320,1152]{3,1,2,0:T(8,128)(2,1)S(1)} %bitcast.24) | data formatting | bytes 23592960
  (17 shorter events, 0.3 us)
Async XLA Ops:
  7.2 2.1 %copy-start = (bf16[1,448,1280]{2,1,0:T(8,128)(2,1)S(1)}, bf16[1,448,1280]{2,1,0:T(8,128)(2,1)}, u32[]{:S(2)}) copy-start(bf16[1,448,1280]{2,1,0:T(8,128)(2,1)} %param.6) | copy-start | bytes 3440644
  7.2 72.5 %reduce-scatter.4.cloned.1.call-start = ((), (), s32[]{:S(2)}) async-start(), calls=%async_computation.3 | async-start | bytes 3686400
  19.4 122.4 %all-gather.2.cloned.1.call-start = ((), (), s32[]{:S(2)}) async-start(), calls=%async_computation.2 | async-start | bytes 3686400 | tf_op jit(solution)/shard_map/all_gather | solution.py:48
  19.4 13.6 %copy-start.2 = (f32[16,32]{1,0:T(8,128)S(1)}, f32[16,32]{1,0:T(8,128)}, u32[]{:S(2)}) copy-start(f32[16,32]{1,0:T(8,128)} %param.9) | copy-start | bytes 6148
  19.5 13.6 %copy-start.3 = (s32[4]{0:T(128)S(1)}, s32[4]{0:T(128)}, u32[]{:S(2)}) copy-start(s32[4]{0:T(128)} %param.10) | copy-start | bytes 52
  82.2 64.4 %collective-permute-start = (bf16[1,320,1152]{2,1,0:T(8,128)(2,1)S(1)}, bf16[1,320,1152]{2,1,0:T(8,128)(2,1)S(1)}, u32[]{:S(2)}, u32[]{:S(2)}) collective-permute-start(bf16[1,320,1152]{2,1,0:T(8,128)(2,1)S(1)} %copy.15), channel_id=1, source_target_pairs={{0,1},{1,2},{2,3},{3,0},{4,5},{5,6},{6,7},{7,4},{8,9},{9,10},{10,1... | collective-permute-start | bytes 2211848 | tf_op jit(solution)/shard_map/ppermute | solution.py:79
  82.3 64.8 %collective-permute-start.1 = (bf16[1,320,1152]{2,1,0:T(8,128)(2,1)S(1)}, bf16[1,320,1152]{2,1,0:T(8,128)(2,1)S(1)}, u32[]{:S(2)}, u32[]{:S(2)}) collective-permute-start(bf16[1,320,1152]{2,1,0:T(8,128)(2,1)S(1)} %copy.15), channel_id=1, source_target_pairs={{0,3},{1,0},{2,1},{3,2},{4,7},{5,4},{6,5},{7,6},{8,11},{9,8},{10,9... | collective-permute-start | bytes 2211848 | tf_op jit(solution)/shard_map/ppermute | solution.py:84
  146.6 10.9 %collective-permute-start.2 = (bf16[1,320,1152]{2,1,0:T(8,128)(2,1)S(1)}, bf16[1,320,1152]{2,1,0:T(8,128)(2,1)S(1)}, u32[]{:S(2)}, u32[]{:S(2)}) collective-permute-start(bf16[1,320,1152]{2,1,0:T(8,128)(2,1)S(1)} %collective-permute-done), channel_id=1, source_target_pairs={{0,1},{1,2},{2,3},{3,0},{4,5},{5,6},{6,7},{7,4},{8,9},{9,10},{10,1... | collective-permute-start | bytes 2211848 | tf_op jit(solution)/shard_map/ppermute | solution.py:79
  171.1 5.3 %copy-start.1 = (bf16[1,448,1280]{2,1,0:T(8,128)(2,1)S(1)}, bf16[1,448,1280]{2,1,0:T(8,128)(2,1)}, u32[]{:S(2)}) copy-start(bf16[1,448,1280]{2,1,0:T(8,128)(2,1)} %param.6) | copy-start | bytes 3440644
Sparse Core Ops, SparseCore 0:
  19.5 60.0 reduce-scatter.3
  81.8 59.9 all-gather.1
